TPU v7x, 32 devices: a whole 2x2x4 slice. The times are simulated.
32 devices in a mesh: row: 8 (over y, x, core), col: 4 (over z).
Axes of the slice: x: 2, y: 2, z: 4, core: 2. Of those that a mesh axis runs over, the one named last changes fastest.
Arguments:
- layer_input: bfloat16 [256, 6144], P('row', 'col'), may hold values from -6 to 6
- norm_gain_rows: float32 [2, 6144], P(None, 'col'), may hold values from 0.1 to 1.9
- norm_bias_rows: float32 [2, 6144], P(None, 'col'), may hold values from -3 to 3
- query_key_value_weight: bfloat16 [6144, 3, 6144], P('col', None, 'row'), may hold values from -0.078125 to 0.078125
- adapter_down_maps: bfloat16 [64, 16, 6144], P(None, None, 'col'), may hold values from -0.078125 to 0.078125
- adapter_up_maps: bfloat16 [64, 16, 3, 6144], P(None, None, None, 'row'), may hold values from -6.5 to 6.5
- output_projection: bfloat16 [6144, 6144], P('row', 'col'), may hold values from -0.078125 to 0.078125
- up_projection: bfloat16 [6144, 24576], P('col', 'row'), may hold values from -0.078125 to 0.078125
- down_projection: bfloat16 [24576, 6144], P('row', 'col'), may hold values from -0.0390625 to 0.0390625
- prompt_token_length: int32 [4], replicated, may hold values from 1 to 64, 160 in all
- adapter_index: int32 [4], replicated, may hold values from 0 to 63
- prompt_page_map: int32 [4], replicated, may hold values from 0 to 3, each once
Outputs:
- new_hidden: bfloat16 [256, 6144], P('row', 'col')
- kv_pages: bfloat16 [4, 2, 64, 6144], P('col', None, None, 'row')
Inputs may be any that keep to these rules, and one draw needn't show every extreme that they name: `prompt_page_map`: each page is named by exactly one prompt. `prompt_token_length`: the prompts together hold 4 * 64 * 5 // 8 real tokens; some prompt fills all 64 positions.
All inputs are finite; a program needn't handle non-finite values.
Results may differ from a plain program's by a relative error of at most 0.023.
Values may be sent and summed in bfloat16 or wider, within the bound.
A program may use at most 128 MiB of HBM per device.

v0:
```python
import jax
import jax.numpy as jnp
from jax import lax
from jax.sharding import PartitionSpec as P

MODEL_WIDTH = 6144
HD = 96
ROT = 24


def normalize(hidden_f32, moments, gain_row, bias_row):
    row_mean = (moments[0] / MODEL_WIDTH)[:, None]
    row_var = (moments[1] / MODEL_WIDTH)[:, None] - row_mean * row_mean
    return ((hidden_f32 - row_mean) * lax.rsqrt(row_var + 1e-05) * gain_row + bias_row).astype(
        jnp.bfloat16
    )


def rotate(heads_in, positions):
    half_rot = ROT // 2
    inv_freq = 10000.0 ** (-jnp.arange(half_rot, dtype=jnp.float32) * 2.0 / ROT)
    angles = positions.astype(jnp.float32)[:, None] * inv_freq[None, :]
    cosine = jnp.cos(angles)[:, None, :]
    sine_part = jnp.sin(angles)[:, None, :]
    front_part = heads_in[..., :half_rot]
    back_part = heads_in[..., half_rot:ROT]
    return jnp.concatenate(
        [
            front_part * cosine - back_part * sine_part,
            back_part * cosine + front_part * sine_part,
            heads_in[..., ROT:],
        ],
        axis=-1,
    )


def per_device(
    layer_input,
    norm_gain_rows,
    norm_bias_rows,
    query_key_value_weight,
    adapter_down_maps,
    adapter_up_maps,
    output_projection,
    up_projection,
    down_projection,
    prompt_token_length,
    adapter_index,
    prompt_page_map,
):
    col_width = layer_input.shape[1]
    hidden_f32 = layer_input.astype(jnp.float32)
    moments = lax.psum(
        (jnp.sum(hidden_f32, axis=-1), jnp.sum(hidden_f32 * hidden_f32, axis=-1)), "col"
    )
    normed_attn = normalize(hidden_f32, moments, norm_gain_rows[0], norm_bias_rows[0])
    normed_mlp = normalize(hidden_f32, moments, norm_gain_rows[1], norm_bias_rows[1])
    normed_attn, normed_mlp = (
        lax.all_gather(normed_attn, "row", axis=0, tiled=True),
        lax.all_gather(normed_mlp, "row", axis=0, tiled=True),
    )
    col_count = lax.axis_size("col")
    prompt_span = normed_attn.shape[0] // col_count
    wide_weight = query_key_value_weight.reshape(col_width, -1)
    query_key_value_width = wide_weight.shape[1]
    adapter_wide_term = adapter_up_maps.reshape(
        adapter_up_maps.shape[0], adapter_up_maps.shape[1], query_key_value_width
    )
    slot_index = jnp.arange(col_count, dtype=jnp.int32)
    token_blocks = normed_attn.reshape(col_count, prompt_span, col_width)
    prompt = lax.axis_index("col")
    tok_slice = token_blocks.reshape(lax.axis_size("col") * prompt_span, col_width)
    base_term = jnp.dot(tok_slice, wide_weight, preferred_element_type=jnp.float32)
    selected_adapter = jnp.take(adapter_index, slot_index, axis=0)
    select_down = adapter_down_maps[selected_adapter]
    select_up = adapter_wide_term[selected_adapter]
    low_rank = jnp.einsum(
        "pld,prd->plr", token_blocks, select_down, preferred_element_type=jnp.float32
    ).astype(jnp.bfloat16)
    extra_term = jnp.einsum("plr,prk->plk", low_rank, select_up, preferred_element_type=jnp.float32)
    qkv_rows = lax.psum_scatter(
        (
            base_term
            + extra_term.reshape(lax.axis_size("col") * prompt_span, query_key_value_width)
        ).astype(jnp.bfloat16),
        "col",
        scatter_dimension=0,
        tiled=True,
    ).astype(jnp.float32)
    local_heads = query_key_value_width // (3 * HD)
    qkv_rows = qkv_rows.reshape(prompt_span, 3, local_heads, HD)
    positions = jnp.arange(prompt_span, dtype=jnp.int32)
    prompt_len = lax.dynamic_slice_in_dim(prompt_token_length, prompt, 1, 0)[0]
    live_mask = positions < prompt_len
    query = rotate(qkv_rows[:, 0], positions).astype(jnp.bfloat16)
    key_rows = rotate(qkv_rows[:, 1], positions).astype(jnp.bfloat16)
    value_rows = qkv_rows[:, 2].astype(jnp.bfloat16)
    zero_key = jnp.zeros_like(key_rows)
    key_rows = jnp.where(live_mask[:, None, None], key_rows, zero_key)
    value_rows = jnp.where(live_mask[:, None, None], value_rows, zero_key)
    scores = jnp.einsum(
        "qhe,khe->hqk", query, key_rows, preferred_element_type=jnp.float32
    ) / jnp.sqrt(jnp.float32(HD))
    allowed = (positions[None, :] <= positions[:, None]) & live_mask[None, :]
    scores = jnp.where(allowed[None, :, :], scores, jnp.float32(-1e30))
    top_score = jnp.max(scores, axis=-1, keepdims=True)
    expo = jnp.exp(scores - top_score)
    probs = (expo / jnp.sum(expo, axis=-1, keepdims=True)).astype(jnp.bfloat16)
    attended = jnp.einsum(
        "hqk,khe->qhe", probs, value_rows, preferred_element_type=jnp.float32
    ).astype(jnp.bfloat16)
    attended = attended.reshape(prompt_span, local_heads * HD)
    page_local = jnp.stack(
        [key_rows.reshape(prompt_span, -1), value_rows.reshape(prompt_span, -1)], axis=0
    )[None]
    target_hit = (prompt_page_map == prompt).astype(jnp.bfloat16)
    kv_pages = jnp.einsum(
        "p,pslk->slk",
        target_hit,
        lax.all_gather(page_local, "col", axis=0, tiled=True),
        preferred_element_type=jnp.float32,
    )[None].astype(jnp.bfloat16)
    tok_slice = normed_mlp
    up_rows = lax.psum_scatter(
        jnp.dot(tok_slice, up_projection, preferred_element_type=jnp.float32).astype(jnp.bfloat16),
        "col",
        scatter_dimension=0,
        tiled=True,
    ).astype(jnp.float32)
    hidden = jax.nn.gelu(up_rows, approximate=False).astype(jnp.bfloat16)
    attn_whole, hidden_whole = (
        lax.all_gather(attended, "col", axis=0, tiled=True),
        lax.all_gather(hidden, "col", axis=0, tiled=True),
    )
    branch = lax.psum_scatter(
        (
            jnp.dot(attn_whole, output_projection, preferred_element_type=jnp.float32)
            + jnp.dot(hidden_whole, down_projection, preferred_element_type=jnp.float32)
        ).astype(jnp.bfloat16),
        "row",
        scatter_dimension=0,
        tiled=True,
    ).astype(jnp.float32)
    new_hidden = (layer_input.astype(jnp.float32) + branch).astype(jnp.bfloat16)
    return (new_hidden, kv_pages)


def solution(mesh):
    return jax.shard_map(
        per_device,
        mesh=mesh,
        in_specs=(
            P("row", "col"),
            P(None, "col"),
            P(None, "col"),
            P("col", None, "row"),
            P(None, None, "col"),
            P(None, None, None, "row"),
            P("row", "col"),
            P("col", "row"),
            P("row", "col"),
            P(),
            P(),
            P(),
        ),
        out_specs=(P("row", "col"), P("col", None, None, "row")),
        check_vma=False,
    )
```

profile of v0, /device:TPU:0, one launch (start us, length us, event | category | flops | bytes accessed | tf_op | source)
XLA Modules:
  0.0 197.1 jit_solution(14919838215069900529)
XLA Ops:
  7.2 1.2 convert_reduce_fusion
  8.4 13.5 %all-reduce = (f32[32]{0:T(128)S(1)}, f32[32]{0:T(128)S(1)}) all-reduce(f32[32]{0:T(128)S(1)} %get-tuple-element.3, f32[32]{0:T(128)S(1)} %get-tuple-element.2), channel_id=1, replica_groups=mesh['row'=8,'col'=4] {'col'}, use_global_device_ids=true, to_apply=%region_3.0 | all-reduce | flops 64 | bytes 512 | tf_op jit(solution)/shard_map/psum | solution.py:53
  21.9 0.9 slice_reduce_fusion.2
  22.7 1.0 fusion.45
  23.8 10.4 %all_gather.17 = bf16[256,1536]{1,0:T(8,128)(2,1)S(1)} all-gather(bf16[32,1536]{1,0:T(8,128)(2,1)S(1)} %get-tuple-element.17), channel_id=1, replica_groups=mesh['row'=8,'col'=4] {'row'}, dimensions={0}, use_global_device_ids=true | all-gather | bytes 884736 | tf_op jit(solution)/shard_map/all_gather | solution.py:60
  34.2 7.4 %convolution_convert_fusion = bf16[256,3072]{1,0:T(8,128)(2,1)} fusion(bf16[256,1536]{1,0:T(8,128)(2,1)S(1)} %all_gather.17, bf16[1536,3072]{1,0:T(8,128)(2,1)} %param.19), kind=kOutput, calls=%fused_computation.6 | convolution fusion | flops 2416705536 | bytes 11796480 | tf_op jit(solution)/shard_map/dot_general | solution.py:125
  41.6 0.0 reduce-scatter.4.cloned.1.call-start
  41.7 4.8 %copy.43 = bf16[64,3,2,8,768]{4,3,1,2,0:T(8,128)(2,1)} copy(bf16[64,3,2,8,768]{4,3,2,1,0:T(8,128)(2,1)} %bitcast.55) | data formatting | bytes 9437184 | tf_op jit(solution)/shard_map/reshape | solution.py:66
  46.5 0.6 gather_fusion
  47.1 2.9 %gather_fusion.2 = bf16[4,16,2304]{2,1,0:T(8,128)(2,1)S(1)} fusion(bf16[64,16,2304]{2,1,0:T(8,128)(2,1)} %bitcast.54, s32[1024]{0:T(1024)S(1)} %pad_clamp_fusion), kind=kCustom, calls=%fused_computation.2 | custom fusion | bytes 589840 | tf_op jit(solution)/shard_map/gather | solution.py:76
  50.0 1.2 gather_fusion.1
  51.3 10.3 %copy.27 = bf16[1536,3,768]{0,2,1:T(8,128)(2,1)} copy(bf16[1536,3,768]{2,0,1:T(8,128)(2,1)} %param.15) | data formatting | bytes 14155776 | tf_op args[3]
  61.6 10.4 %all_gather.15 = bf16[256,1536]{1,0:T(8,128)(2,1)S(1)} all-gather(bf16[32,1536]{1,0:T(8,128)(2,1)S(1)} %get-tuple-element.16), channel_id=1, replica_groups=mesh['row'=8,'col'=4] {'row'}, dimensions={0}, use_global_device_ids=true | all-gather | bytes 884736 | tf_op jit(solution)/shard_map/all_gather | solution.py:59
  72.0 1.7 fusion.7
  73.6 6.2 %fusion.1 = bf16[256,2304]{1,0:T(8,128)(2,1)} fusion(f32[256,2304]{1,0:T(8,128)S(1)} %bitcast.61, bf16[256,1536]{1,0:T(8,128)(2,1)S(1)} %all_gather.15, bf16[1536,2304]{0,1:T(8,128)(2,1)} %bitcast.53), kind=kOutput, calls=%fused_computation.5 | convolution fusion | flops 1813118976 | bytes 11403264 | tf_op jit(solution)/shard_map/dot_general | solution.py:73
  79.9 0.6 dynamic_slice.3
  80.5 3.4 %fusion.9 = bf16[64,3072]{1,0:T(8,128)(2,1)} fusion(bf16[64,3072]{1,0:T(8,128)(2,1)} %reduce-scatter.6.cloned.1.call-done), kind=kLoop, calls=%fused_computation.21 | loop fusion | flops 12976128 | bytes 786432 | tf_op jit(solution)/shard_map/convert_element_type | solution.py:130
  84.0 0.7 iota_compare_fusion.1
  84.7 0.1 fusion.62
  84.7 0.2 multiply_cosine_fusion
  84.9 21.5 %reduce-scatter.4.cloned.1.call-done = bf16[64,2304]{1,0:T(8,128)(2,1)} async-done(((bf16[256,2304]{1,0:T(8,128)(2,1)}), bf16[64,2304]{1,0:T(8,128)(2,1)}) %reduce-scatter.4.cloned.1.call-update) | async-done | bytes 294928 | tf_op jit(solution)/shard_map/reduce_scatter | solution.py:81
  106.4 1.5 reshape.213
  108.0 0.1 copy.57
  108.1 0.1 slice.67
  108.2 0.1 copy.58
  108.2 0.1 slice.81
  108.3 0.1 multiply_subtract_fusion
  108.5 0.1 maximum_convert_fusion
  108.7 0.1 subtract_convert_fusion
  108.8 0.3 fusion.80
  109.1 0.3 fusion.4
  109.4 0.3 fusion.6
  109.7 0.1 copy.33
  109.8 0.1 reshape.211
  109.9 17.8 %all_gather.16 = bf16[256,768]{1,0:T(8,128)(2,1)S(1)} all-gather(bf16[64,768]{1,0:T(8,128)(2,1)S(1)} %reshape.211), channel_id=1, replica_groups=mesh['row'=8,'col'=4] {'col'}, dimensions={0}, use_global_device_ids=true | all-gather | bytes 491520 | tf_op jit(solution)/shard_map/all_gather | solution.py:132
  127.8 19.5 %all-gather.3.cloned.1.call-done = bf16[256,3072]{1,0:T(8,128)(2,1)} async-done(((bf16[64,3072]{1,0:T(8,128)(2,1)}), bf16[256,3072]{1,0:T(8,128)(2,1)}) %all-gather.3.cloned.1.call-update) | async-done | bytes 1572880 | tf_op jit(solution)/shard_map/all_gather | solution.py:133
  147.2 5.6 %fusion.86 = f32[256,1536]{1,0:T(8,128)S(1)} fusion(bf16[256,3072]{1,0:T(8,128)(2,1)} %all-gather.3.cloned.1.call-done, bf16[3072,1536]{1,0:T(8,128)(2,1)} %param.20), kind=kOutput, calls=%fused_computation.124 | convolution fusion | flops 2415919104 | bytes 12582912 | tf_op jit(solution)/shard_map/dot_general | solution.py:138
  152.9 1.7 fusion.2
  154.6 0.1 copy.34
  154.7 0.8 convert_element_type.121
  155.5 0.1 copy.35
  155.6 0.1 convert_element_type.122
  155.7 1.1 broadcast_select_fusion.1
  156.9 18.0 %all-gather = bf16[8,64,768]{2,1,0:T(8,128)(2,1)S(1)} all-gather(bf16[2,64,768]{2,1,0:T(8,128)(2,1)S(1)} %pad_maximum_fusion), channel_id=2, replica_groups=mesh['row'=8,'col'=4] {'col'}, dimensions={0}, use_global_device_ids=true | all-gather | bytes 983040 | tf_op jit(solution)/shard_map/all_gather | solution.py:120
  175.0 0.7 fusion.39
  175.7 0.7 copy.59
  176.4 12.7 %reduce-scatter.8.cloned.1.call-done = bf16[32,1536]{1,0:T(8,128)(2,1)} async-done(((bf16[256,1536]{1,0:T(8,128)(2,1)}), bf16[32,1536]{1,0:T(8,128)(2,1)}) %reduce-scatter.8.cloned.1.call-update) | async-done | bytes 98320 | tf_op jit(solution)/shard_map/reduce_scatter | solution.py:135
  189.1 1.6 fusion.49
  (33 shorter events, 0.4 us)
Async XLA Ops:
  7.2 42.9 %copy-start = (bf16[64,16,1536]{2,1,0:T(8,128)(2,1)S(1)}, bf16[64,16,1536]{2,1,0:T(8,128)(2,1)}, u32[]{:S(2)}) copy-start(bf16[64,16,1536]{2,1,0:T(8,128)(2,1)} %param.16) | copy-start | bytes 9437188
  7.2 73.3 %reduce-scatter.6.cloned.1.call-start = ((), (), s32[]{:S(2)}) async-start(), calls=%async_computation.4 | async-start | bytes 1966080 | tf_op jit(solution)/shard_map/reduce_scatter | solution.py:124
  41.6 64.8 %reduce-scatter.4.cloned.1.call-start = ((), (), s32[]{:S(2)}) async-start(), calls=%async_computation.3 | async-start | bytes 1474560 | tf_op jit(solution)/shard_map/reduce_scatter | solution.py:81
  41.7 4.8 %copy-start.2 = (s32[4]{0:T(128)S(1)}, s32[4]{0:T(128)}, u32[]{:S(2)}) copy-start(s32[4]{0:T(128)} %param.22) | copy-start | bytes 52
  73.6 6.3 %copy-start.5 = (s32[4]{0:T(128)S(1)}, s32[4]{0:T(128)}, u32[]{:S(2)}) copy-start(s32[4]{0:T(128)} %param.21) | copy-start | bytes 52
  79.8 67.4 %all-gather.3.cloned.1.call-start = ((), (), s32[]{:S(2)}) async-start(), calls=%async_computation.5 | async-start | bytes 1966080 | tf_op jit(solution)/shard_map/all_gather | solution.py:133
  83.9 105.1 %reduce-scatter.8.cloned.1.call-start = ((), (), s32[]{:S(2)}) async-start(), calls=%async_computation.6 | async-start | bytes 884736 | tf_op jit(solution)/shard_map/reduce_scatter | solution.py:135
  127.8 25.1 %copy-start.3 = (bf16[768,1536]{1,0:T(8,128)(2,1)S(1)}, bf16[768,1536]{1,0:T(8,128)(2,1)}, u32[]{:S(2)}) copy-start(bf16[768,1536]{1,0:T(8,128)(2,1)} %param.18) | copy-start | bytes 7077892
  154.6 20.4 %copy-start.6 = (s32[4]{0:T(128)S(1)}, s32[4]{0:T(128)}, u32[]{:S(2)}) copy-start(s32[4]{0:T(128)} %param.23) | copy-start | bytes 52
  155.5 33.5 %copy-start.4 = (bf16[32,1536]{1,0:T(8,128)(2,1)S(1)}, bf16[32,1536]{1,0:T(8,128)(2,1)}, u32[]{:S(2)}) copy-start(bf16[32,1536]{1,0:T(8,128)(2,1)} %param.12) | copy-start | bytes 294916
  155.5 35.1 %copy-start.1 = (bf16[64,16,1536]{2,1,0:T(8,128)(2,1)S(1)}, bf16[64,16,1536]{2,1,0:T(8,128)(2,1)}, u32[]{:S(2)}) copy-start(bf16[64,16,1536]{2,1,0:T(8,128)(2,1)} %param.16) | copy-start | bytes 9437188
Sparse Core Ops, SparseCore 0:
  41.7 32.5 reduce-scatter.5
  79.9 26.4 reduce-scatter.3
  108.0 39.1 all-gather.2
  154.7 34.2 reduce-scatter.7
where the time goes:
time: 198 us; the launch traced here: 197 us
  blocking collectives  70.1 us (35%)
  waiting for transfers between devices  53.7 us (27%)
  local copies, waits for them, and re-layouts  25.3 us (13%)
  matrix products  24.1 us (12%)
  between operations  14 us (7%)
  other arithmetic  9.75 us (5%)
    reduce_scatter x1, waiting for transfers between devices, per_device(): lax.psum_scatter((base_term + extra_term.reshape(lax.axis_size('col') * p...  21.5 us
    all_gather x1, waiting for transfers between devices, per_device(): lax.all_gather(hidden, 'col', axis=0, tiled=True)  19.5 us
    all_gather x1, blocking collectives, per_device(): lax.all_gather(page_local, 'col', axis=0, tiled=True)  18 us
    all_gather x1, blocking collectives, per_device(): lax.all_gather(attended, 'col', axis=0, tiled=True)  17.8 us
    psum x1, blocking collectives, per_device(): lax.psum((jnp.sum(hidden_f32, axis=-1), jnp.sum(hidden_f32 * hidden_f32,...  13.5 us
    reduce_scatter x1, waiting for transfers between devices, per_device(): lax.psum_scatter((jnp.dot(attn_whole, output_projection, preferred_elemen...  12.7 us
    unnamed x18, local copies, waits for them, and re-layouts  10.5 us
    all_gather x1, blocking collectives, per_device(): lax.all_gather(normed_mlp, 'row', axis=0, tiled=True)  10.4 us
  transfers between devices with their start and end apart: 4, of which 3 were waited for; matrix products, arithmetic and copies ran while one was open for 20% of the time, Pallas kernels for 0%

commit v1 on v0

--- a/solution.py
+++ b/solution.py
@@ -1,6 +1,11 @@
+import functools
+
 import jax
 import jax.numpy as jnp
+import numpy as np
 from jax import lax
+from jax.experimental import pallas as pl
+from jax.experimental.pallas import tpu as pltpu
 from jax.sharding import PartitionSpec as P
 
 MODEL_WIDTH = 6144
@@ -145,9 +150,468 @@
     return (new_hidden, kv_pages)
 
 
+MESH = pl.DeviceIdType.MESH
+F32 = jnp.float32
+BF16 = jnp.bfloat16
+
+
+def remote(src, dst, send_sem, recv_sem, device):
+    return pltpu.make_async_remote_copy(
+        src_ref=src,
+        dst_ref=dst,
+        send_sem=send_sem,
+        recv_sem=recv_sem,
+        device_id=device,
+        device_id_type=MESH,
+    )
+
+
+def fused_kernel(
+    R, C, K, UC, LAG,
+    x_ref, gain_ref, bias_ref, wq_hbm, ad_hbm, au_hbm, wo_hbm, wu_hbm, wd_hbm,
+    cos_ref, sa_ref, sb_ref, hm_ref, len_ref, aidx_ref, pmap_ref,
+    out_ref, kv_ref,
+    wq, ad, au, wo, wu, wd,
+    xg, mom, momr, st, xn0, xn1, xs, low, qp, rx, qs,
+    part, inp, pairb, hid, attb, ao, acc, br, sbuf, cb, rb,
+    w_sem, x_send, x_recv, m_send, m_recv, t_send, t_recv, q_send, q_recv,
+    p_send, p_recv, h_send, h_recv, a_send, a_recv, s_send, s_recv, b_send, b_recv,
+):
+    r = lax.axis_index("row")
+    c = lax.axis_index("col")
+    par = lax.rem(r, 2)
+    chip = lax.div(r, 2)
+    sib = r + 1 - 2 * par
+    H = R // 2
+    TR, D = x_ref.shape
+    S = (R * TR) // C
+    W3 = qs.shape[2]
+    per = S // TR
+
+    loads = [
+        pltpu.make_async_copy(a, b, w_sem.at[i])
+        for i, (a, b) in enumerate(
+            [(wq_hbm, wq), (ad_hbm, ad), (au_hbm, au), (wu_hbm, wu), (wo_hbm, wo), (wd_hbm, wd)]
+        )
+    ]
+    for ld in loads:
+        ld.start()
+
+    barrier = pltpu.get_barrier_semaphore()
+    for i in range(1, R):
+        pl.semaphore_signal(barrier, inc=1, device_id={"row": lax.rem(r + i, R)}, device_id_type=MESH)
+    for i in range(1, C):
+        pl.semaphore_signal(barrier, inc=1, device_id={"col": lax.rem(c + i, C)}, device_id_type=MESH)
+    pl.semaphore_wait(barrier, R - 1 + C - 1)
+
+    def x_peer(i):
+        return remote(x_ref, xg.at[r], x_send.at[i], x_recv.at[r], {"row": lax.rem(r + 2 * i, R)})
+
+    def x_sib(i):
+        src = lax.rem(r + 2 * i, R)
+        buf = x_ref if i == 0 else xg.at[src]
+        return remote(buf, xg.at[src], x_send.at[H + i], x_recv.at[src], {"row": sib})
+
+    for i in range(1, H):
+        x_peer(i).start()
+    x_sib(0).start()
+
+    xf = x_ref[...].astype(F32)
+    lane = lax.broadcasted_iota(jnp.int32, (TR, 128), 1)
+    s1 = jnp.sum(xf, axis=1, keepdims=True)
+    s2 = jnp.sum(xf * xf, axis=1, keepdims=True)
+    mom[...] = jnp.where(lane == 0, s1, s2)
+
+    def m_peer(i):
+        return remote(mom, momr.at[c], m_send.at[i], m_recv.at[c], {"col": lax.rem(c + i, C)})
+
+    def m_from(i):
+        src = lax.rem(c + i, C)
+        return remote(mom, momr.at[src], m_send.at[i], m_recv.at[src], {"col": src})
+
+    for i in range(1, C):
+        m_peer(i).start()
+    xg[r] = x_ref[...]
+    for i in range(1, C):
+        m_from(i).wait_recv()
+    tot = mom[...]
+    for i in range(1, C):
+        tot = tot + momr[lax.rem(c + i, C)]
+    st[r] = tot
+
+    def t_peer(i):
+        return remote(st.at[r], st.at[r], t_send.at[i], t_recv.at[r], {"row": lax.rem(r + i, R)})
+
+    for i in range(1, R):
+        t_peer(i).start()
+    for i in range(1, H):
+        src = lax.rem(r + 2 * i, R)
+        remote(x_ref, xg.at[src], x_send.at[i], x_recv.at[src], {"row": src}).wait_recv()
+        x_sib(i).start()
+
+    for src in range(R):
+        @pl.when(r != src)
+        def _():
+            remote(st.at[src], st.at[src], t_send.at[0], t_recv.at[src], {"row": sib}).wait_recv()
+
+        @pl.when(lax.rem(r + src, 2) == 1)
+        def _():
+            remote(xg.at[src], xg.at[src], x_send.at[0], x_recv.at[src], {"row": sib}).wait_recv()
+
+        mean = st[src][:, 0:1] / MODEL_WIDTH
+        var = st[src][:, 1:2] / MODEL_WIDTH - mean * mean
+        z = (xg[src].astype(F32) - mean) * lax.rsqrt(var + 1e-05)
+        xn0[src // per, pl.ds((src % per) * TR, TR), :] = (z * gain_ref[0:1, :] + bias_ref[0:1, :]).astype(BF16)
+        xn1[pl.ds(src * TR, TR), :] = (z * gain_ref[1:2, :] + bias_ref[1:2, :]).astype(BF16)
+
+    inv = []
+    for s in range(C):
+        v = jnp.int32(0)
+        for p in range(1, C):
+            v = jnp.where(pmap_ref[p] == s, p, v)
+        inv.append(v)
+    for s in range(C):
+        xs[pl.ds(s * S, S), :] = xn0[inv[s]]
+    loads[0].wait()
+    loads[1].wait()
+    loads[2].wait()
+    for s in range(C):
+        low[s] = lax.dot_general(
+            xs[pl.ds(s * S, S), :], ad[aidx_ref[inv[s]]], (((1,), (1,)), ((), ())),
+            preferred_element_type=F32,
+        ).astype(BF16)
+
+    def q_right(d, j):
+        return remote(qp.at[d, j], rx.at[0, d, j], q_send.at[d, j], q_recv.at[0, d, j], {"col": lax.rem(c + 1, C)})
+
+    def q_left(d, j):
+        return remote(qp.at[d, j], rx.at[1, d, j], q_send.at[d, j], q_recv.at[1, d, j], {"col": lax.rem(c + C - 1, C)})
+
+    for j in range(3):
+        base = jnp.dot(xs[...], wq[j], preferred_element_type=F32)
+        for s in range(C):
+            extra = jnp.dot(low[s], au[aidx_ref[inv[s]], j], preferred_element_type=F32)
+            qp[s, j] = (base[s * S:(s + 1) * S] + extra).astype(BF16)
+
+        @pl.when(c == 0)
+        def _():
+            for d in range(C - 1, 0, -1):
+                q_right(d, j).start()
+
+        @pl.when(c == C - 1)
+        def _():
+            for d in range(C - 1):
+                q_left(d, j).start()
+
+    loads[3].wait()
+    end = jnp.logical_or(c == 0, c == C - 1)
+    middle = jnp.logical_not(end)
+    inner = jnp.where(c < C // 2, c + 1, c - 1)
+    outer = jnp.where(c == 1, 0, C - 1)
+
+    def p_copy(k):
+        return remote(part.at[k], inp.at[k], p_send.at[k], p_recv.at[k], {"col": inner})
+
+    def h_copy(k):
+        return remote(hid.at[k], hid.at[k], h_send.at[k], h_recv.at[k], {"col": outer})
+
+    def up_term(k):
+        cols = pl.ds(pl.multiple_of(k * UC, UC), UC)
+        part[k] = jnp.dot(xn1[...], wu[:, cols], preferred_element_type=F32).astype(BF16)
+
+        @pl.when(end)
+        def _():
+            p_copy(k).start()
+
+    def up_loop(k, carry):
+        up_term(k)
+        return carry
+
+    lax.fori_loop(0, LAG, up_loop, 0)
+
+    for j in range(3):
+        for kk in range(C - 1):
+            d = C - 1 - kk
+
+            @pl.when(jnp.logical_and(c > 0, c < d))
+            def _():
+                q_right(d, j).wait_recv()
+                qp[d, j] = (qp[d, j].astype(F32) + rx[0, d, j].astype(F32)).astype(BF16)
+                q_right(d, j).start()
+
+            e = kk
+
+            @pl.when(jnp.logical_and(c < C - 1, c > e))
+            def _():
+                q_left(e, j).wait_recv()
+                qp[e, j] = (qp[e, j].astype(F32) + rx[1, e, j].astype(F32)).astype(BF16)
+                q_left(e, j).start()
+
+    for j in range(3):
+        qs[j] = qp[c, j].astype(F32)
+
+        @pl.when(c > 0)
+        def _():
+            q_right(c, j).wait_recv()
+            qs[j] = qs[j] + rx[0, c, j].astype(F32)
+
+        @pl.when(c < C - 1)
+        def _():
+            q_left(c, j).wait_recv()
+            qs[j] = qs[j] + rx[1, c, j].astype(F32)
+
+    def rot(v):
+        return (
+            v * cos_ref[...]
+            + pltpu.roll(v, W3 - ROT // 2, 1) * sa_ref[...]
+            + pltpu.roll(v, ROT // 2, 1) * sb_ref[...]
+        )
+
+    mine = jnp.int32(0)
+    for p in range(1, C):
+        mine = jnp.where(pmap_ref[p] == c, p, mine)
+    length = len_ref[mine]
+    live = lax.broadcasted_iota(jnp.int32, (S, W3), 0) < length
+    query = rot(qs[0]).astype(BF16)
+    key = jnp.where(live, rot(qs[1]), 0.0).astype(BF16)
+    value = jnp.where(live, qs[2], 0.0).astype(BF16)
+    kv_ref[0, 0] = key
+    kv_ref[0, 1] = value
+    qi = lax.broadcasted_iota(jnp.int32, (S, S), 0)
+    ki = lax.broadcasted_iota(jnp.int32, (S, S), 1)
+    allowed = jnp.logical_and(ki <= qi, ki < length)
+    att = jnp.zeros((S, W3), F32)
+    for h in range(W3 // HD):
+        mask = hm_ref[h:h + 1, :]
+        scores = lax.dot_general(
+            query * mask.astype(BF16), key, (((1,), (1,)), ((), ())), preferred_element_type=F32
+        ) / np.float32(np.sqrt(np.float32(HD)))
+        scores = jnp.where(allowed, scores, -1e30)
+        expo = jnp.exp(scores - jnp.max(scores, axis=1, keepdims=True))
+        probs = (expo / jnp.sum(expo, axis=1, keepdims=True)).astype(BF16)
+        att = att + jnp.dot(probs, value, preferred_element_type=F32) * mask
+    attb[c] = att.astype(BF16)
+
+    def a_right(s):
+        return remote(attb.at[s], attb.at[s], a_send.at[0, s], a_recv.at[s], {"col": lax.rem(c + 1, C)})
+
+    def a_left(s):
+        return remote(attb.at[s], attb.at[s], a_send.at[1, s], a_recv.at[s], {"col": lax.rem(c + C - 1, C)})
+
+    @pl.when(c < C - 1)
+    def _():
+        a_right(c).start()
+
+    @pl.when(c > 0)
+    def _():
+        a_left(c).start()
+
+    def att_round(t):
+        for s in range(C):
+            @pl.when(c == s + t)
+            def _():
+                a_right(s).wait_recv()
+                if s + t < C - 1:
+                    a_right(s).start()
+
+            @pl.when(c == s - t)
+            def _():
+                a_left(s).wait_recv()
+                if s - t > 0:
+                    a_left(s).start()
+
+    loads[4].wait()
+    loads[5].wait()
+    acc[...] = jnp.zeros_like(acc)
+
+    def down(k):
+        rows = pl.ds(pl.multiple_of(k * UC, UC), UC)
+        acc[...] += jnp.dot(hid[k], wd[rows, :], preferred_element_type=F32)
+
+    def main(k, carry):
+        @pl.when(k + LAG < K)
+        def _():
+            up_term(k + LAG)
+
+        @pl.when(jnp.logical_and(middle, k < K))
+        def _():
+            p_copy(k).wait_recv()
+            part[k] = (part[k].astype(F32) + inp[k].astype(F32)).astype(BF16)
+            remote(part.at[k], pairb.at[k], p_send.at[k], h_recv.at[k], {"col": inner}).start()
+
+        @pl.when(k >= 1)
+        def _():
+            m = k - 1
+
+            @pl.when(middle)
+            def _():
+                remote(part.at[m], pairb.at[m], p_send.at[m], h_recv.at[m], {"col": inner}).wait_recv()
+                u = part[m].astype(F32) + pairb[m].astype(F32)
+                hid[m] = (0.5 * u * (1.0 + lax.erf(u * np.float32(np.sqrt(0.5))))).astype(BF16)
+                h_copy(m).start()
+
+            @pl.when(end)
+            def _():
+                remote(hid.at[m], hid.at[m], h_send.at[m], h_recv.at[m], {"col": inner}).wait_recv()
+
+            down(m)
+
+        return carry
+
+    bounds = [0] + [K * (t + 1) // (C + 1) + 1 for t in range(1, C)] + [K + 1]
+    for t in range(1, C + 1):
+        lax.fori_loop(bounds[t - 1], bounds[t], main, 0)
+        if t < C:
+            att_round(t)
+        if t == C - 1:
+            for p in range(C):
+                ao[pl.ds(p * S, S), :] = attb[pmap_ref[p]]
+            acc[...] += jnp.dot(ao[...], wo[...], preferred_element_type=F32)
+
+    for d in range(R):
+        br[d] = acc[pl.ds(d * TR, TR), :].astype(BF16)
+
+    def s_copy(i):
+        j = lax.rem(chip + i, H)
+        return remote(br.at[2 * j + 1 - par], sbuf.at[j], s_send.at[i], s_recv.at[j], {"row": sib})
+
+    def b_copy(i):
+        j = lax.rem(chip + i, H)
+        return remote(cb.at[j], rb.at[chip], b_send.at[i], b_recv.at[chip], {"row": 2 * j + par})
+
+    def from_sib(i):
+        j = lax.rem(chip + i, H)
+        remote(sbuf.at[j], sbuf.at[j], s_send.at[i], s_recv.at[j], {"row": sib}).wait_recv()
+        return br[2 * j + par].astype(F32) + sbuf[j].astype(F32)
+
+    order = list(range(1, H)) + [0]
+    for i in order:
+        s_copy(i).start()
+    for i in range(1, H):
+        cb[lax.rem(chip + i, H)] = from_sib(i).astype(BF16)
+        b_copy(i).start()
+    total = from_sib(0)
+    for i in range(1, H):
+        src = lax.rem(chip + i, H)
+        remote(cb.at[src], rb.at[src], b_send.at[i], b_recv.at[src], {"row": 2 * src + par}).wait_recv()
+        total = total + rb[src].astype(F32)
+    out_ref[...] = (x_ref[...].astype(F32) + total).astype(BF16)
+
+    for i in range(1, H):
+        x_peer(i).wait_send()
+        b_copy(i).wait_send()
+    for i in range(H):
+        x_sib(i).wait_send()
+        s_copy(i).wait_send()
+    for i in range(1, C):
+        m_peer(i).wait_send()
+    for i in range(1, R):
+        t_peer(i).wait_send()
+    for j in range(3):
+        for d in range(C):
+            @pl.when(c != d)
+            def _():
+                q_right(d, j).wait_send()
+    for s in range(C):
+        @pl.when(jnp.logical_and(s <= c, c < C - 1))
+        def _():
+            a_right(s).wait_send()
+
+        @pl.when(jnp.logical_and(s >= c, c > 0))
+        def _():
+            a_left(s).wait_send()
+
+    def drain(k, carry):
+        p_copy(k).wait_send()
+
+        @pl.when(middle)
+        def _():
+            h_copy(k).wait_send()
+
+        return carry
+
+    lax.fori_loop(0, K, drain, 0)
+
+
+def rotary_tables(span, width):
+    half = ROT // 2
+    inv_freq = np.float32(10000.0) ** (-np.arange(half, dtype=np.float32) * np.float32(2.0) / np.float32(ROT))
+    angles = np.arange(span, dtype=np.float32)[:, None] * inv_freq[None, :].astype(np.float32)
+    cosine, sine = np.cos(angles), np.sin(angles)
+    cos = np.ones((span, width), np.float32)
+    front = np.zeros((span, width), np.float32)
+    back = np.zeros((span, width), np.float32)
+    for low in range(0, width, HD):
+        cos[:, low:low + half] = cosine
+        cos[:, low + half:low + ROT] = cosine
+        front[:, low:low + half] = -sine
+        back[:, low + half:low + ROT] = sine
+    heads = (np.arange(width)[None, :] // HD == np.arange(width // HD)[:, None]).astype(np.float32)
+    return cos, front, back, heads
+
+
+def fused(
+    layer_input, norm_gain_rows, norm_bias_rows, query_key_value_weight, adapter_down_maps,
+    adapter_up_maps, output_projection, up_projection, down_projection, prompt_token_length,
+    adapter_index, prompt_page_map,
+):
+    R, C = lax.axis_size("row"), lax.axis_size("col")
+    TR, D = layer_input.shape
+    T = TR * R
+    S = T // C
+    W3 = query_key_value_weight.shape[2]
+    U = up_projection.shape[1]
+    UC = 256
+    K = U // UC
+    H = R // 2
+    wq = jnp.transpose(query_key_value_weight, (1, 0, 2))
+    au = jnp.transpose(adapter_up_maps, (0, 2, 1, 3))
+    tables = [jnp.asarray(t) for t in rotary_tables(S, W3)]
+    vm = pl.BlockSpec(memory_space=pltpu.VMEM)
+    sm = pl.BlockSpec(memory_space=pltpu.SMEM)
+    hbm = pl.BlockSpec(memory_space=pl.ANY)
+    dma = pltpu.SemaphoreType.DMA
+    V = pltpu.VMEM
+    return pl.pallas_call(
+        functools.partial(fused_kernel, R, C, K, UC, 6),
+        out_shape=(
+            jax.ShapeDtypeStruct((TR, D), BF16),
+            jax.ShapeDtypeStruct((1, 2, S, W3), BF16),
+        ),
+        in_specs=[vm] * 3 + [hbm] * 6 + [vm] * 4 + [sm] * 3,
+        out_specs=(vm, vm),
+        scratch_shapes=[
+            V(wq.shape, BF16), V(adapter_down_maps.shape, BF16), V(au.shape, BF16),
+            V(output_projection.shape, BF16), V(up_projection.shape, BF16), V(down_projection.shape, BF16),
+            V((R, TR, D), BF16), V((TR, 128), F32), V((C, TR, 128), F32), V((R, TR, 128), F32),
+            V((C, S, D), BF16), V((T, D), BF16), V((T, D), BF16), V((C, S, au.shape[2]), BF16),
+            V((C, 3, S, W3), BF16), V((2, C, 3, S, W3), BF16), V((3, S, W3), F32),
+            V((K, T, UC), BF16), V((K, T, UC), BF16), V((K, T, UC), BF16), V((K, T, UC), BF16),
+            V((C, S, W3), BF16), V((T, W3), BF16), V((T, D), F32),
+            V((R, TR, D), BF16), V((H, TR, D), BF16), V((H, TR, D), BF16), V((H, TR, D), BF16),
+            dma((6,)), dma((R,)), dma((R,)), dma((C,)), dma((C,)), dma((R,)), dma((R,)),
+            dma((C, 3)), dma((2, C, 3)), dma((K,)), dma((K,)), dma((K,)), dma((K,)),
+            dma((2, C)), dma((C,)), dma((H,)), dma((H,)), dma((H,)), dma((H,)),
+        ],
+        compiler_params=pltpu.CompilerParams(
+            collective_id=0, has_side_effects=True, vmem_limit_bytes=63 * 1024 * 1024
+        ),
+    )(
+        layer_input, norm_gain_rows, norm_bias_rows, wq, adapter_down_maps, au,
+        output_projection, up_projection, down_projection, *tables,
+        prompt_token_length, adapter_index, prompt_page_map,
+    )
+
+
+def layer(*args):
+    weight, up = args[3], args[7]
+    fits = lax.axis_size("col") == 4 and weight.shape[2] % 128 == 0 and up.shape[1] % 256 == 0
+    return fused(*args) if fits and weight.shape[0] % 128 == 0 else per_device(*args)
+
+
 def solution(mesh):
     return jax.shard_map(
-        per_device,
+        layer,
         mesh=mesh,
         in_specs=(
             P("row", "col"),

time: 198 us -> 112 us (0.57)
  Pallas kernels: 0 us -> 108 us
  blocking collectives: 70.1 us -> 0 us
  waiting for transfers between devices: 53.7 us -> 0 us
  matrix products: 24.1 us -> 0 us
  local copies, waits for them, and re-layouts: 25.3 us -> 3.16 us
  between operations: 14 us -> 0.64 us
  other arithmetic: 9.75 us -> 0 us
    pallas_call x0 -> x1, Pallas kernels: none -> 108 us  [fused(): pl.pallas_call(functools.partial(fused_kernel, R, C, K, UC, 6), out_shape...]
    all_gather x4 -> x0, blocking collectives: 56.6 us -> none  [the longest x1 18 us: per_device(): lax.all_gather(page_local, 'col', axis=0, tiled=True)]
    reduce_scatter x3 -> x0, waiting for transfers between devices: 34.2 us -> none  [the longest x1 21.5 us: per_device(): lax.psum_scatter((base_term + extra_term.reshape(lax.axis_size('col') * p...]
    dot_general x8 -> x0, matrix products: 23.8 us -> none  [the longest x1 7.42 us: per_device(): jnp.dot(tok_slice, up_projection, preferred_element_type=jnp.float32)]
    all_gather x1 -> x0, waiting for transfers between devices: 19.5 us -> none  [per_device(): lax.all_gather(hidden, 'col', axis=0, tiled=True)]
    psum x1 -> x0, blocking collectives: 13.5 us -> none  [per_device(): lax.psum((jnp.sum(hidden_f32, axis=-1), jnp.sum(hidden_f32 * hidden_f32,...]
    unnamed x18 -> x2, local copies, waits for them, and re-layouts: 10.5 us -> 3.16 us
    reshape x3 -> x0, local copies, waits for them, and re-layouts: 6.43 us -> none  [the longest x1 4.77 us: per_device(): adapter_up_maps.reshape(adapter_up_maps.shape[0], adapter_up_maps.shape[1...]
  transfers between devices with their start and end apart: 4 -> 0, of which waited for: 3 -> 0; matrix products, arithmetic and copies ran while one was open for 20% -> 0% of each run, Pallas kernels for 0% -> 0%
where the time goes in v1:
time: 112 us
  Pallas kernels  108 us (96%)
  local copies, waits for them, and re-layouts  3.16 us (3%)
    pallas_call x1, Pallas kernels, fused(): pl.pallas_call(functools.partial(fused_kernel, R, C, K, UC, 6), out_shape...  108 us
    unnamed x2, local copies, waits for them, and re-layouts  3.16 us

profile of v1, /device:TPU:0, one launch (start us, length us, event | category | flops | bytes accessed | tf_op | source)
XLA Modules:
  0.0 111.8 jit_solution(11602294759888279059)
XLA Ops:
  0.6 108.0 %shard_map.167 = (bf16[32,1536]{1,0:T(8,128)(2,1)}, bf16[1,2,64,768]{3,2,1,0:T(8,128)(2,1)}) custom-call(bf16[32,1536]{1,0:T(8,128)(2,1)} %x_ref.1, f32[2,1536]{1,0:T(2,128)} %gain_ref.1, f32[2,1536]{1,0:T(2,128)} %bias_ref.1, bf16[3,1536,768]{2,1,0:T(8,128)(2,1)} %bitcast.2, bf16[64,16,1536]{2,1,0:T(8,128)(2,1)} %ad_hbm.1, ...), custom_call_target="tpu_custom_call" | custom-call | tf_op jit(solution)/shard_map/pallas_call | solution.py:575
  108.6 1.5 %copy.20 = bf16[32,1536]{1,0:T(8,128)(2,1)} copy(bf16[32,1536]{1,0:T(8,128)(2,1)} %get-tuple-element.4) | data formatting | bytes 196608
  110.2 1.6 %copy.21 = bf16[1,2,64,768]{3,2,1,0:T(8,128)(2,1)} copy(bf16[1,2,64,768]{3,2,1,0:T(8,128)(2,1)} %get-tuple-element.5) | data formatting | bytes 393216
